TPU v7x, 512 devices: a whole 4x4x16 slice. The times are simulated.
512 devices in a mesh: ctx: 32 (over x, z_lo, core), tp: 16 (over y, z_hi).
Axes of the slice: x: 4, y: 4, z: 16 (z_hi: 4, z_lo: 4; z = z_hi * 4 + z_lo), core: 2. Of those that a mesh axis runs over, the one named last changes fastest.
Arguments:
- attention_out: bfloat16 [512, 8192], P('ctx', 'tp'), may hold values from -6 to 6
- w_out: bfloat16 [8192, 8192], P('tp', 'ctx'), may hold values from -0.0625 to 0.0625
- residual: bfloat16 [512, 8192], P(('ctx', 'tp')), may hold values from -6 to 6
- norm_gain: float32 [8192], replicated, may hold values from 0.1 to 1.9
- w_gate: bfloat16 [28672, 8192], P(('ctx', 'tp')), may hold values from -0.0625 to 0.0625
- w_up: bfloat16 [28672, 8192], P(('ctx', 'tp')), may hold values from -0.0625 to 0.0625
- w_down: bfloat16 [32, 896, 8192], P(None, 'tp', 'ctx'), may hold values from -0.03125 to 0.03125
Outputs:
- mixed: bfloat16 [512, 8192], P(('ctx', 'tp'))
All inputs are finite; a program needn't handle non-finite values.
Results may differ from a plain program's by a relative error of at most 0.02.
Values may be sent and summed in bfloat16 or wider, within the bound.
No kernel may reach another device: no remote copies, remote signals or barrier semaphores. Data moves between devices by JAX's collectives and lax.ppermute only.
A program may use at most 64 MiB of HBM per device.

v0:
```python
import jax
import jax.numpy as jnp
from jax import lax
from jax.sharding import PartitionSpec as P


def owner_order(partial_value, ctx_count, tp_count, row_count):
    col_count = partial_value.shape[1]
    grouped = partial_value.reshape(ctx_count, tp_count, row_count, col_count)
    return jnp.transpose(grouped, (1, 0, 2, 3)).reshape(tp_count * ctx_count * row_count, col_count)


def shards(attention_out, w_out, residual, norm_gain, w_gate, w_up, w_down):
    row_count = residual.shape[0]
    ctx_count = lax.axis_size("ctx")
    tp_count = lax.axis_size("tp")
    unit_count = w_gate.shape[0]
    col_count = w_down.shape[2]
    partial_value = jnp.dot(
        lax.all_gather(attention_out, "ctx", axis=0, tiled=True),
        w_out,
        preferred_element_type=jnp.float32,
    )
    summed = lax.psum_scatter(
        owner_order(partial_value, ctx_count, tp_count, row_count).astype(jnp.bfloat16),
        "tp",
        scatter_dimension=0,
        tiled=True,
    ).astype(jnp.float32)
    proj = lax.all_to_all(
        summed.astype(jnp.bfloat16), "ctx", split_axis=0, concat_axis=1, tiled=True
    ).astype(summed.dtype)
    carried = residual.astype(jnp.float32) + proj
    mean_square = jnp.mean(carried * carried, axis=-1, keepdims=True)
    normed = (carried * lax.rsqrt(mean_square + 1e-05) * norm_gain).astype(jnp.bfloat16)
    paired = jnp.concatenate([w_gate, w_up], axis=0)
    group = lax.all_gather(normed, "tp", axis=0, tiled=True)
    gate_up = lax.dot_general(
        lax.all_gather(group, "ctx", axis=0, tiled=True),
        paired,
        (((1,), (1,)), ((), ())),
        preferred_element_type=jnp.float32,
    )
    gate_part = gate_up[:, :unit_count]
    up_part = gate_up[:, unit_count:]
    hidden = (jax.nn.silu(gate_part) * up_part).astype(jnp.bfloat16)
    flat_down = w_down.reshape(ctx_count * unit_count, col_count)
    partial_down = jnp.dot(
        lax.all_gather(hidden, "ctx", axis=1, tiled=True),
        flat_down,
        preferred_element_type=jnp.float32,
    )
    reduced = lax.psum_scatter(
        owner_order(partial_down, ctx_count, tp_count, row_count).astype(jnp.bfloat16),
        "tp",
        scatter_dimension=0,
        tiled=True,
    ).astype(jnp.float32)
    down = lax.all_to_all(
        reduced.astype(jnp.bfloat16), "ctx", split_axis=0, concat_axis=1, tiled=True
    ).astype(reduced.dtype)
    return (carried + down).astype(jnp.bfloat16)


def solution(mesh):
    in_specs = (
        P("ctx", "tp"),
        P("tp", "ctx"),
        P(("ctx", "tp"), None),
        P(),
        P(("ctx", "tp"), None),
        P(("ctx", "tp"), None),
        P(None, "tp", "ctx"),
    )
    out_specs = P(("ctx", "tp"), None)
    return jax.shard_map(shards, mesh=mesh, in_specs=in_specs, out_specs=out_specs, check_vma=False)
```

profile of v0, /device:TPU:1, one launch (start us, length us, event | category | flops | bytes accessed | tf_op | source)
XLA Modules:
  0.0 513.3 jit_solution(6987445112993718375)
XLA Ops:
  6.5 0.0 copy-start
  6.5 0.0 copy-start.1
  6.5 0.0 copy-start.2
  6.5 0.0 reduce-scatter.3.cloned.1.call-start
  6.5 48.2 %all_gather.12 = bf16[512,512]{1,0:T(8,128)(2,1)S(1)} all-gather(bf16[16,512]{1,0:T(8,128)(2,1)} %param.7), channel_id=1, replica_groups=mesh['ctx'=32,'tp'=16] {'ctx'}, dimensions={0}, use_global_device_ids=true | all-gather | bytes 540672 | tf_op jit(solution)/shard_map/all_gather | solution.py:20
  54.7 0.0 copy-start.3
  54.7 0.0 copy-start.4
  54.7 1.4 convolution_convert_fusion.1
  56.1 0.8 copy.12
  56.9 0.0 reduce-scatter.3.cloned.1.call-update
  56.9 0.0 all-gather.4.cloned.1.call-start
  56.9 108.8 %reduce-scatter.3.cloned.1.call-done = bf16[32,256]{1,0:T(8,128)(2,1)} async-done(((bf16[512,256]{1,0:T(8,128)(2,1)}), bf16[32,256]{1,0:T(8,128)(2,1)}) %reduce-scatter.3.cloned.1.call-update) | async-done | bytes 16400 | tf_op jit(solution)/shard_map/reduce_scatter | solution.py:24
  165.8 0.5 broadcast.4
  166.3 1.4 reduce.1
  167.6 14.4 %all_to_all.26 = bf16[32,2,128]{2,1,0:T(2,128)(2,1)S(1)} all-to-all(bf16[32,2,128]{2,1,0:T(2,128)(2,1)S(1)} %reshape.72), channel_id=1, replica_groups=mesh['ctx'=32,'tp'=16] {'ctx'}, dimensions={0} | all-to-all | bytes 32768 | tf_op jit(solution)/shard_map/all_to_all | solution.py:30
  182.0 0.0 copy-done.1
  182.1 0.7 multiply_reduce_fusion
  183.5 0.0 copy-done.2
  183.5 0.1 convert_bitcast_fusion
  183.6 50.3 %all-gather = bf16[16,1,8192]{2,1,0:T(2,128)(2,1)S(1)} all-gather(bf16[1,1,8192]{2,1,0:T(2,128)(2,1)S(1)} %convert_bitcast_fusion), channel_id=1, replica_groups=mesh['ctx'=32,'tp'=16] {'tp'}, dimensions={0}, use_global_device_ids=true | all-gather | bytes 278528 | tf_op jit(solution)/shard_map/all_gather | solution.py:37
  233.9 1.0 copy.19
  234.9 0.0 all-gather.4.cloned.1.call-update
  234.9 0.0 all-gather.6.cloned.1.call-start
  235.0 71.6 %all-gather.4.cloned.1.call-done = bf16[512,8192]{1,0:T(8,128)(2,1)} async-done(((bf16[16,8192]{1,0:T(8,128)(2,1)}), bf16[512,8192]{1,0:T(8,128)(2,1)}) %all-gather.4.cloned.1.call-update) | async-done | bytes 8388624 | tf_op jit(solution)/shard_map/all_gather | solution.py:39
  306.5 0.0 copy-done.3
  306.5 0.0 copy-done.4
  306.5 6.2 %fusion = f32[512,112]{0,1:T(8,128)S(1)} fusion(bf16[512,8192]{1,0:T(8,128)(2,1)} %all-gather.4.cloned.1.call-done, bf16[56,8192]{1,0:T(8,128)(2,1)S(1)} %copy-done.3, bf16[56,8192]{1,0:T(8,128)(2,1)S(1)} %copy-done.4), kind=kOutput, calls=%fused_computation | convolution fusion | flops 943194112 | bytes 10452992 | tf_op jit(solution)/shard_map/dot_general | solution.py:38
  312.8 0.7 fusion.5
  313.4 0.0 all-gather.6.cloned.1.call-update
  313.5 0.0 reduce-scatter.5.cloned.1.call-start
  313.5 64.0 %all-gather.6.cloned.1.call-done = bf16[512,1792]{0,1:T(8,128)(2,1)} async-done(((bf16[512,56]{0,1:T(8,128)(2,1)}), bf16[512,1792]{0,1:T(8,128)(2,1)}) %all-gather.6.cloned.1.call-update) | async-done | bytes 1835024 | tf_op jit(solution)/shard_map/all_gather | solution.py:49
  377.5 2.8 copy.14
  380.3 0.0 copy-done
  380.3 0.6 fusion.4
  380.9 0.8 copy.15
  381.7 0.0 reduce-scatter.5.cloned.1.call-update
  381.7 108.5 %reduce-scatter.5.cloned.1.call-done = bf16[32,256]{1,0:T(8,128)(2,1)} async-done(((bf16[512,256]{1,0:T(8,128)(2,1)}), bf16[32,256]{1,0:T(8,128)(2,1)}) %reduce-scatter.5.cloned.1.call-update) | async-done | bytes 16400 | tf_op jit(solution)/shard_map/reduce_scatter | solution.py:53
  490.3 1.4 reduce.2
  491.6 14.4 %all_to_all.27 = bf16[32,2,128]{2,1,0:T(2,128)(2,1)S(1)} all-to-all(bf16[32,2,128]{2,1,0:T(2,128)(2,1)S(1)} %reshape.74), channel_id=1, replica_groups=mesh['ctx'=32,'tp'=16] {'ctx'}, dimensions={0} | all-to-all | bytes 32768 | tf_op jit(solution)/shard_map/all_to_all | solution.py:59
  506.1 0.7 fusion.6
  (4 shorter events, 0.1 us)
Async XLA Ops:
  6.5 373.7 %copy-start = (bf16[32,56,256]{2,1,0:T(8,128)(2,1)S(1)}, bf16[32,56,256]{2,1,0:T(8,128)(2,1)}, u32[]{:S(2)}) copy-start(bf16[32,56,256]{2,1,0:T(8,128)(2,1)} %param.13) | copy-start | bytes 2752516
  6.5 175.5 %copy-start.1 = (bf16[1,8192]{1,0:T(2,128)(2,1)S(1)}, bf16[1,8192]{1,0:T(2,128)(2,1)}, u32[]{:S(2)}) copy-start(bf16[1,8192]{1,0:T(2,128)(2,1)} %param.9) | copy-start | bytes 49156
  6.5 176.9 %copy-start.2 = (f32[8192]{0:T(1024)S(1)}, f32[8192]{0:T(1024)}, u32[]{:S(2)}) copy-start(f32[8192]{0:T(1024)} %param.10) | copy-start | bytes 98308
  6.5 159.2 %reduce-scatter.3.cloned.1.call-start = ((), (), s32[]{:S(2)}) async-start(), calls=%async_computation.4 | async-start | bytes 278528 | tf_op jit(solution)/shard_map/reduce_scatter | solution.py:24
  54.7 251.8 %copy-start.3 = (bf16[56,8192]{1,0:T(8,128)(2,1)S(1)}, bf16[56,8192]{1,0:T(8,128)(2,1)}, u32[]{:S(2)}) copy-start(bf16[56,8192]{1,0:T(8,128)(2,1)} %param.12) | copy-start | bytes 2752516
  54.7 251.8 %copy-start.4 = (bf16[56,8192]{1,0:T(8,128)(2,1)S(1)}, bf16[56,8192]{1,0:T(8,128)(2,1)}, u32[]{:S(2)}) copy-start(bf16[56,8192]{1,0:T(8,128)(2,1)} %param.11) | copy-start | bytes 2752516
  56.9 249.6 %all-gather.4.cloned.1.call-start = ((), (), s32[]{:S(2)}) async-start(), calls=%async_computation.5 | async-start | bytes 8650752 | tf_op jit(solution)/shard_map/all_gather | solution.py:39
  234.9 142.6 %all-gather.6.cloned.1.call-start = ((), (), s32[]{:S(2)}) async-start(), calls=%async_computation.6 | async-start | bytes 1892352 | tf_op jit(solution)/shard_map/all_gather | solution.py:49
  313.5 176.8 %reduce-scatter.5.cloned.1.call-start = ((), (), s32[]{:S(2)}) async-start(), calls=%async_computation.7 | async-start | bytes 278528 | tf_op jit(solution)/shard_map/reduce_scatter | solution.py:53
Sparse Core Ops, SparseCore 0:
  57.0 108.6 reduce-scatter.2
  235.0 71.4 all-gather.3
  313.6 63.8 all-gather.5
  381.9 108.2 reduce-scatter.4
where the time goes:
time: 514 us; the launch traced here: 513 us
  waiting for transfers between devices  353 us (69%)
  blocking collectives  127 us (25%)
  between operations  13.9 us (3%)
  matrix products  8.23 us (2%)
  local copies, waits for them, and re-layouts  5.9 us (1%)
    reduce_scatter x1, waiting for transfers between devices, shards(): lax.psum_scatter(owner_order(partial_value, ctx_count, tp_count, row_coun...  109 us
    reduce_scatter x1, waiting for transfers between devices, shards(): lax.psum_scatter(owner_order(partial_down, ctx_count, tp_count, row_count...  109 us
    all_gather x1, waiting for transfers between devices, shards(): lax.all_gather(group, 'ctx', axis=0, tiled=True)  71.6 us
    all_gather x1, waiting for transfers between devices, shards(): lax.all_gather(hidden, 'ctx', axis=1, tiled=True)  64 us
    all_gather x1, blocking collectives, shards(): group = lax.all_gather(normed, 'tp', axis=0, tiled=True)  50.3 us
    all_gather x1, blocking collectives, shards(): lax.all_gather(attention_out, 'ctx', axis=0, tiled=True)  48.2 us
    all_to_all x1, blocking collectives, shards(): lax.all_to_all(reduced.astype(jnp.bfloat16), 'ctx', split_axis=0, concat_...  14.4 us
    all_to_all x1, blocking collectives, shards(): lax.all_to_all(summed.astype(jnp.bfloat16), 'ctx', split_axis=0, concat_a...  14.4 us
  transfers between devices with their start and end apart: 4, of which 4 were waited for; matrix products, arithmetic and copies ran while one was open for 0% of the time, Pallas kernels for 0%

commit v1 on v0

--- a/solution.py
+++ b/solution.py
@@ -56,8 +56,14 @@
         scatter_dimension=0,
         tiled=True,
     ).astype(jnp.float32)
-    down = lax.all_to_all(
-        reduced.astype(jnp.bfloat16), "ctx", split_axis=0, concat_axis=1, tiled=True
+    down = jnp.concatenate(
+        lax.all_to_all(
+            jnp.stack(jnp.split(reduced.astype(jnp.bfloat16), lax.axis_size("ctx"), axis=0)),
+            "ctx",
+            0,
+            0,
+        ),
+        axis=1,
     ).astype(reduced.dtype)
     return (carried + down).astype(jnp.bfloat16)
 

time: 514 us -> 536 us (1.043)
  local copies, waits for them, and re-layouts: 5.9 us -> 27.9 us
    unnamed x15 -> x46, local copies, waits for them, and re-layouts: 1.09 us -> 22.4 us
where the time goes in v1:
time: 536 us; the launch traced here: 535 us
  waiting for transfers between devices  353 us (66%)
  blocking collectives  127 us (24%)
  local copies, waits for them, and re-layouts  27.9 us (5%)
  between operations  13.9 us (3%)
  matrix products  8.23 us (2%)
    reduce_scatter x1, waiting for transfers between devices, shards(): lax.psum_scatter(owner_order(partial_value, ctx_count, tp_count, row_coun...  109 us
    reduce_scatter x1, waiting for transfers between devices, shards(): lax.psum_scatter(owner_order(partial_down, ctx_count, tp_count, row_count...  109 us
    all_gather x1, waiting for transfers between devices, shards(): lax.all_gather(group, 'ctx', axis=0, tiled=True)  71.6 us
    all_gather x1, waiting for transfers between devices, shards(): lax.all_gather(hidden, 'ctx', axis=1, tiled=True)  64 us
    all_gather x1, blocking collectives, shards(): group = lax.all_gather(normed, 'tp', axis=0, tiled=True)  50.3 us
    all_gather x1, blocking collectives, shards(): lax.all_gather(attention_out, 'ctx', axis=0, tiled=True)  48.2 us
    unnamed x46, local copies, waits for them, and re-layouts  22.4 us
    all_to_all x1, blocking collectives, shards(): lax.all_to_all(jnp.stack(jnp.split(reduced.astype(jnp.bfloat16), lax.axis...  14.4 us
  transfers between devices with their start and end apart: 4, of which 4 were waited for; matrix products, arithmetic and copies ran while one was open for 0% of the time, Pallas kernels for 0%

profile of v1, /device:TPU:1, one launch (start us, length us, event | category | flops | bytes accessed | tf_op | source)
XLA Modules:
  0.0 534.7 jit_solution(765502621927711339)
XLA Ops:
  6.5 0.0 copy-start
  6.5 0.0 reduce-scatter.3.cloned.1.call-start
  6.5 48.2 %all_gather.12 = bf16[512,512]{1,0:T(8,128)(2,1)S(1)} all-gather(bf16[16,512]{1,0:T(8,128)(2,1)} %param.7), channel_id=1, replica_groups=mesh['ctx'=32,'tp'=16] {'ctx'}, dimensions={0}, use_global_device_ids=true | all-gather | bytes 540672 | tf_op jit(solution)/shard_map/all_gather | solution.py:20
  54.7 1.4 convolution_convert_fusion.1
  56.1 0.8 copy.12
  56.9 0.0 reduce-scatter.3.cloned.1.call-update
  56.9 0.0 all-gather.4.cloned.1.call-start
  56.9 108.8 %reduce-scatter.3.cloned.1.call-done = bf16[32,256]{1,0:T(8,128)(2,1)} async-done(((bf16[512,256]{1,0:T(8,128)(2,1)}), bf16[32,256]{1,0:T(8,128)(2,1)}) %reduce-scatter.3.cloned.1.call-update) | async-done | bytes 16400 | tf_op jit(solution)/shard_map/reduce_scatter | solution.py:24
  165.8 0.5 broadcast.4
  166.3 1.4 reduce.1
  167.6 14.4 %all_to_all.18 = bf16[32,2,128]{2,1,0:T(2,128)(2,1)S(1)} all-to-all(bf16[32,2,128]{2,1,0:T(2,128)(2,1)S(1)} %reshape.67), channel_id=1, replica_groups=mesh['ctx'=32,'tp'=16] {'ctx'}, dimensions={0} | all-to-all | bytes 32768 | tf_op jit(solution)/shard_map/all_to_all | solution.py:30
  182.1 0.7 multiply_reduce_fusion
  183.5 0.1 convert_bitcast_fusion
  183.6 50.3 %all-gather = bf16[16,1,8192]{2,1,0:T(2,128)(2,1)S(1)} all-gather(bf16[1,1,8192]{2,1,0:T(2,128)(2,1)S(1)} %convert_bitcast_fusion), channel_id=1, replica_groups=mesh['ctx'=32,'tp'=16] {'tp'}, dimensions={0}, use_global_device_ids=true | all-gather | bytes 278528 | tf_op jit(solution)/shard_map/all_gather | solution.py:37
  233.9 1.0 copy.18
  234.9 0.0 all-gather.4.cloned.1.call-update
  234.9 0.0 all-gather.6.cloned.1.call-start
  235.0 71.6 %all-gather.4.cloned.1.call-done = bf16[512,8192]{1,0:T(8,128)(2,1)} async-done(((bf16[16,8192]{1,0:T(8,128)(2,1)}), bf16[512,8192]{1,0:T(8,128)(2,1)}) %all-gather.4.cloned.1.call-update) | async-done | bytes 8388624 | tf_op jit(solution)/shard_map/all_gather | solution.py:39
  306.5 6.2 %fusion = f32[512,112]{0,1:T(8,128)S(1)} fusion(bf16[512,8192]{1,0:T(8,128)(2,1)} %all-gather.4.cloned.1.call-done, bf16[56,8192]{1,0:T(8,128)(2,1)S(1)} %copy-done.3, bf16[56,8192]{1,0:T(8,128)(2,1)S(1)} %copy-done.4), kind=kOutput, calls=%fused_computation | convolution fusion | flops 943194112 | bytes 10452992 | tf_op jit(solution)/shard_map/dot_general | solution.py:38
  312.8 0.7 fusion.5
  313.4 0.0 all-gather.6.cloned.1.call-update
  313.5 0.0 reduce-scatter.5.cloned.1.call-start
  313.5 64.0 %all-gather.6.cloned.1.call-done = bf16[512,1792]{0,1:T(8,128)(2,1)} async-done(((bf16[512,56]{0,1:T(8,128)(2,1)}), bf16[512,1792]{0,1:T(8,128)(2,1)}) %all-gather.6.cloned.1.call-update) | async-done | bytes 1835024 | tf_op jit(solution)/shard_map/all_gather | solution.py:49
  377.5 2.8 copy.14
  380.3 0.0 copy-done
  380.3 0.6 fusion.4
  380.9 0.8 copy.15
  381.7 0.0 reduce-scatter.5.cloned.1.call-update
  381.7 108.5 %reduce-scatter.5.cloned.1.call-done = bf16[32,256]{1,0:T(8,128)(2,1)} async-done(((bf16[512,256]{1,0:T(8,128)(2,1)}), bf16[32,256]{1,0:T(8,128)(2,1)}) %reduce-scatter.5.cloned.1.call-update) | async-done | bytes 16400 | tf_op jit(solution)/shard_map/reduce_scatter | solution.py:53
  490.3 0.7 constant_dynamic-update-slice_fusion.31
  490.9 0.7 constant_dynamic-update-slice_fusion.30
  491.6 0.7 constant_dynamic-update-slice_fusion.29
  492.3 0.7 constant_dynamic-update-slice_fusion.28
  493.0 0.7 constant_dynamic-update-slice_fusion.27
  493.7 0.7 constant_dynamic-update-slice_fusion.26
  494.4 0.7 constant_dynamic-update-slice_fusion.25
  495.1 0.7 constant_dynamic-update-slice_fusion.24
  495.8 0.7 constant_dynamic-update-slice_fusion.23
  496.4 0.7 constant_dynamic-update-slice_fusion.22
  497.1 0.7 constant_dynamic-update-slice_fusion.21
  497.8 0.7 constant_dynamic-update-slice_fusion.20
  498.5 0.7 constant_dynamic-update-slice_fusion.19
  499.2 0.7 constant_dynamic-update-slice_fusion.18
  499.9 0.7 constant_dynamic-update-slice_fusion.17
  500.5 0.7 constant_dynamic-update-slice_fusion.16
  501.2 0.7 constant_dynamic-update-slice_fusion.15
  501.9 0.7 constant_dynamic-update-slice_fusion.14
  502.6 0.7 constant_dynamic-update-slice_fusion.13
  503.3 0.7 constant_dynamic-update-slice_fusion.12
  504.0 0.7 constant_dynamic-update-slice_fusion.11
  504.7 0.7 constant_dynamic-update-slice_fusion.10
  505.4 0.7 constant_dynamic-update-slice_fusion.9
  506.1 0.7 constant_dynamic-update-slice_fusion.8
  506.8 0.7 constant_dynamic-update-slice_fusion.7
  507.4 0.7 constant_dynamic-update-slice_fusion.6
  508.1 0.7 constant_dynamic-update-slice_fusion.5
  508.8 0.7 constant_dynamic-update-slice_fusion.4
  509.5 0.7 constant_dynamic-update-slice_fusion.3
  510.2 0.7 constant_dynamic-update-slice_fusion.2
  510.9 0.7 constant_dynamic-update-slice_fusion.1
  511.6 0.7 constant_dynamic-update-slice_fusion
  512.3 0.7 reduce.2
  513.1 14.4 %all_to_all.19 = bf16[32,2,128]{2,1,0:T(2,128)(2,1)S(1)} all-to-all(bf16[32,2,128]{2,1,0:T(2,128)(2,1)S(1)} %reshape.69), channel_id=1, replica_groups=mesh['ctx'=32,'tp'=16] {'ctx'}, dimensions={0} | all-to-all | bytes 32768 | tf_op jit(solution)/shard_map/all_to_all | solution.py:60
  527.5 0.7 fusion.6
  (12 shorter events, 0.1 us)
Async XLA Ops:
  6.5 373.7 %copy-start = (bf16[32,56,256]{2,1,0:T(8,128)(2,1)S(1)}, bf16[32,56,256]{2,1,0:T(8,128)(2,1)}, u32[]{:S(2)}) copy-start(bf16[32,56,256]{2,1,0:T(8,128)(2,1)} %param.13) | copy-start | bytes 2752516
  6.5 175.5 %copy-start.1 = (bf16[1,8192]{1,0:T(2,128)(2,1)S(1)}, bf16[1,8192]{1,0:T(2,128)(2,1)}, u32[]{:S(2)}) copy-start(bf16[1,8192]{1,0:T(2,128)(2,1)} %param.9) | copy-start | bytes 49156
  6.5 176.9 %copy-start.2 = (f32[8192]{0:T(1024)S(1)}, f32[8192]{0:T(1024)}, u32[]{:S(2)}) copy-start(f32[8192]{0:T(1024)} %param.10) | copy-start | bytes 98308
  6.5 159.2 %reduce-scatter.3.cloned.1.call-start = ((), (), s32[]{:S(2)}) async-start(), calls=%async_computation.4 | async-start | bytes 278528 | tf_op jit(solution)/shard_map/reduce_scatter | solution.py:24
  54.7 251.8 %copy-start.3 = (bf16[56,8192]{1,0:T(8,128)(2,1)S(1)}, bf16[56,8192]{1,0:T(8,128)(2,1)}, u32[]{:S(2)}) copy-start(bf16[56,8192]{1,0:T(8,128)(2,1)} %param.12) | copy-start | bytes 2752516
  54.7 251.8 %copy-start.4 = (bf16[56,8192]{1,0:T(8,128)(2,1)S(1)}, bf16[56,8192]{1,0:T(8,128)(2,1)}, u32[]{:S(2)}) copy-start(bf16[56,8192]{1,0:T(8,128)(2,1)} %param.11) | copy-start | bytes 2752516
  56.9 249.6 %all-gather.4.cloned.1.call-start = ((), (), s32[]{:S(2)}) async-start(), calls=%async_computation.5 | async-start | bytes 8650752 | tf_op jit(solution)/shard_map/all_gather | solution.py:39
  234.9 142.6 %all-gather.6.cloned.1.call-start = ((), (), s32[]{:S(2)}) async-start(), calls=%async_computation.6 | async-start | bytes 1892352 | tf_op jit(solution)/shard_map/all_gather | solution.py:49
  313.5 176.8 %reduce-scatter.5.cloned.1.call-start = ((), (), s32[]{:S(2)}) async-start(), calls=%async_computation.7 | async-start | bytes 278528 | tf_op jit(solution)/shard_map/reduce_scatter | solution.py:53
Sparse Core Ops, SparseCore 0:
  57.0 108.6 reduce-scatter.2
  235.0 71.4 all-gather.3
  313.6 63.8 all-gather.5
  381.9 108.2 reduce-scatter.4
